TPU v7x, 256 devices: a whole 4x4x8 slice. The times are simulated.
256 devices in a mesh: rows: 64 (over y, z, core), cols: 4 (over x).
Axes of the slice: x: 4, y: 4, z: 8, core: 2. Of those that a mesh axis runs over, the one named last changes fastest.
Arguments:
- residual_block: float32 [524288, 64], P('rows', 'cols'), may hold values from -6 to 6
- basis: bfloat16 [524288, 64], P('rows', 'cols'), may hold values from -0.0078125 to 0.0078125
- fine_tiles: bfloat16 [4096, 4, 128, 128], P('rows')
- fine_index: int32 [4096, 4], P('rows'), may hold values from 0 to 4095, as said below
- mid_tiles: bfloat16 [512, 3, 128, 128], P('rows')
- fine_owner: int32 [524288], P('rows'), may hold values from 0 to 65535, as said below
- mid_owner: int32 [65536], P('rows'), may hold values from 0 to 8191, as said below
- coarse_inverse: float32 [8192, 8192], P('rows'), as said below
Outputs:
- directions: float32 [524288, 64], P('rows', 'cols')
- gram: float32 [64, 64], P(None, 'cols')
Inputs may be any that keep to these rules, and one draw needn't show every extreme that they name: `fine_index`: slot 0 of block row g names g itself; every block named in a block row of partition p (block rows p*64 to p*64 + 63) belongs to partition p - 1, p or p + 1. `fine_owner`: the fine vertices of partition p map to level-one rows p*1024 to p*1024 + 1023; every level-one row receives exactly 8 vertices. `mid_owner`: the level-one rows of partitions 2q and 2q + 1 map to level-two rows 2q*128 to 2q*128 + 2*128 - 1; every level-two row receives exactly 8 level-one rows. coarse_inverse is symmetric.
All inputs are finite; a program needn't handle non-finite values.
Results may differ from a plain program's by a relative error of at most 0.013.
Values may be sent and summed in bfloat16 or wider, within the bound.
A program may use at most 64 MiB of HBM per device.

v0:
```python
import jax
import jax.numpy as jnp
from jax import lax
from jax.sharding import PartitionSpec as P

DAMPING = 0.6666666666666666


def with_halo(array, sides, width):
    for axis, dim in sides:
        peers, length = (lax.axis_size(axis), array.shape[dim])
        up = [(i, (i + 1) % peers) for i in range(peers - 1)]
        down = [(j, i) for i, j in up]
        last = lax.slice_in_dim(array, length - width, length, axis=dim)
        leading = lax.slice_in_dim(array, 0, width, axis=dim)
        before = lax.ppermute(last, axis, up)
        after = lax.ppermute(leading, axis, down)
        array = jnp.concatenate([before, array, after], axis=dim)
    return array


def swapped(value, axis, apart):
    mask = 2**apart
    pairs = [(source, source ^ mask) for source in range(lax.axis_size(axis))]
    return lax.ppermute(value, axis, pairs)


def fine_apply(vector, matrix, window_index):
    extent = matrix.shape[2]
    packed = vector.astype(jnp.bfloat16).reshape(-1, extent, vector.shape[1])
    window = with_halo(packed, (("rows", 0),), packed.shape[0])
    picked = window[window_index]
    product = jnp.einsum("bkij,bkjc->bic", matrix, picked, preferred_element_type=jnp.float32)
    return product.reshape(vector.shape)


def mid_apply(vector, matrix):
    blocks = matrix.shape[0]
    extent = matrix.shape[2]
    packed = vector.astype(jnp.bfloat16).reshape(blocks, extent, vector.shape[1])
    window = with_halo(packed, (("rows", 0),), 1)
    product = jnp.einsum(
        "bij,bjc->bic", matrix[:, 0], window[:-2], preferred_element_type=jnp.float32
    )
    product = product + jnp.einsum(
        "bij,bjc->bic", matrix[:, 1], window[1:-1], preferred_element_type=jnp.float32
    )
    product = product + jnp.einsum(
        "bij,bjc->bic", matrix[:, 2], window[2:], preferred_element_type=jnp.float32
    )
    return product.reshape(vector.shape)


def on_device(
    residual_block, basis, fine_tiles, fine_index, mid_tiles, fine_owner, mid_owner, coarse_inverse
):
    device = lax.axis_index("rows")
    blocks = fine_tiles.shape[0]
    mid_count = mid_tiles.shape[0] * mid_tiles.shape[2]
    coarse_count = coarse_inverse.shape[0]
    col_width = residual_block.shape[1]
    parity = device % 2
    window_index = fine_index - (device - 1) * blocks
    fine_local = fine_owner - device * mid_count
    mid_local = mid_owner - (device - parity) * coarse_count
    fine_inv = 1.0 / jnp.diagonal(fine_tiles[:, 0], axis1=1, axis2=2).astype(jnp.float32).reshape(
        -1, 1
    )
    mid_inv = 1.0 / jnp.diagonal(mid_tiles[:, 1], axis1=1, axis2=2).astype(jnp.float32).reshape(
        -1, 1
    )
    fine_x = DAMPING * fine_inv * residual_block
    fine_x = fine_x + DAMPING * fine_inv * (
        residual_block - fine_apply(fine_x, fine_tiles, window_index)
    )
    fine_res = residual_block - fine_apply(fine_x, fine_tiles, window_index)
    partial_mid = jax.ops.segment_sum(fine_res, fine_local, num_segments=mid_count)
    mid_x = DAMPING * mid_inv * partial_mid
    mid_x = mid_x + DAMPING * mid_inv * (partial_mid - mid_apply(mid_x, mid_tiles))
    mid_res = partial_mid - mid_apply(mid_x, mid_tiles)
    partial_value = jax.ops.segment_sum(mid_res, mid_local, num_segments=2 * coarse_count)
    halves = partial_value.reshape(2, coarse_count, col_width)
    own_half = jnp.where(parity == 0, halves[0], halves[1])
    other_half = jnp.where(parity == 0, halves[1], halves[0])
    coarse_rhs = own_half + swapped(other_half, "rows", 0)
    coarse_fix = jnp.dot(
        coarse_inverse,
        lax.all_gather(coarse_rhs, "rows", axis=0, tiled=True),
        precision=lax.Precision.HIGHEST,
        preferred_element_type=jnp.float32,
    )
    partner_fix = swapped(coarse_fix, "rows", 0)
    pair_values = jnp.where(
        parity == 0,
        jnp.concatenate([coarse_fix, partner_fix], axis=0),
        jnp.concatenate([partner_fix, coarse_fix], axis=0),
    )
    mid_x = mid_x + pair_values[mid_local]
    mid_x = mid_x + DAMPING * mid_inv * (partial_mid - mid_apply(mid_x, mid_tiles))
    fine_x = fine_x + mid_x[fine_local]
    finished = fine_x + DAMPING * fine_inv * (
        residual_block - fine_apply(fine_x, fine_tiles, window_index)
    )
    rounded = finished.astype(jnp.bfloat16)
    partial_gram = lax.dot_general(
        lax.all_gather(basis, "cols", axis=1, tiled=True),
        rounded,
        (((0,), (0,)), ((), ())),
        preferred_element_type=jnp.float32,
    )
    gram = lax.psum(partial_gram, "rows")
    return (finished, gram)


def solution(mesh):
    in_specs = (
        P("rows", "cols"),
        P("rows", "cols"),
        P("rows", None, None, None),
        P("rows", None),
        P("rows", None, None, None),
        P("rows"),
        P("rows"),
        P("rows", None),
    )
    out_specs = (P("rows", "cols"), P(None, "cols"))
    return jax.shard_map(
        on_device, mesh=mesh, in_specs=in_specs, out_specs=out_specs, check_vma=False
    )
```

profile of v0, /device:TPU:4, one launch (start us, length us, event | category | flops | bytes accessed | tf_op | source)
XLA Modules:
  0.0 407.9 jit_solution(2754003155523653004)
XLA Ops:
  7.2 1.5 slice-done
  8.8 3.9 copy.204
  12.7 1.9 gather_fusion
  14.8 1.8 collective-permute-start
  16.5 1.3 collective-permute-start.1
  17.9 0.1 copy.163
  18.0 0.1 reshape.105
  18.1 1.0 slice_bitcast_fusion
  19.1 3.1 copy.166
  22.2 1.9 gather_fusion.2
  24.3 0.8 gather_fusion.1
  25.2 5.7 %convolution_bitcast_fusion.2 = f32[64,2,8,128]{3,2,1,0:T(8,128)S(1)} fusion(bf16[64,4,128,16]{2,3,1,0:T(8,128)(2,1)S(1)} %bitcast.177, bf16[64,4,128,128]{3,2,1,0:T(8,128)(2,1)} %param.10), kind=kOutput, calls=%fused_computation.11 | convolution fusion | flops 134217728 | bytes 9961472 | tf_op jit(solution)/shard_map/bkij,bkjc->bic/dot_general | solution.py:33
  30.9 0.1 copy_bitcast_fusion.1
  31.0 4.7 %collective-permute-start.2 = (bf16[64,128,16]{1,2,0:T(8,128)(2,1)S(1)}, bf16[64,128,16]{1,2,0:T(8,128)(2,1)S(1)}, u32[]{:S(2)}, u32[]{:S(2)}) collective-permute-start(bf16[64,128,16]{1,2,0:T(8,128)(2,1)S(1)} %copy_bitcast_fusion.1), channel_id=1, source_target_pairs={{0,4},{4,8},{8,12},{12,16},{16,20},{20,24},{24,28},{28,32},{32,36}... | collective-permute-start | bytes 786440 | tf_op jit(solution)/shard_map/ppermute | solution.py:16
  35.7 1.3 collective-permute-start.3
  37.1 3.3 collective-permute-done.3
  40.5 0.8 gather_fusion.3
  41.3 5.7 %convolution_bitcast_fusion.1 = f32[64,2,8,128]{3,2,1,0:T(8,128)S(1)} fusion(bf16[64,4,128,16]{2,3,1,0:T(8,128)(2,1)S(1)} %bitcast.178, bf16[64,4,128,128]{3,2,1,0:T(8,128)(2,1)} %param.10), kind=kOutput, calls=%fused_computation.10 | convolution fusion | flops 134217728 | bytes 9961472 | tf_op jit(solution)/shard_map/bkij,bkjc->bic/dot_general | solution.py:33
  47.1 2.6 copy.172
  49.7 44.4 %scatter_custom_fusion = f32[1024,16]{1,0:T(8,128)S(1)} fusion(s32[8192]{0:T(1024)S(1)} %get-tuple-element.11, f32[8192,16]{1,0:T(8,128)} %copy.172, f32[]{:T(128)} %constant.25.clone.1), kind=kCustom, calls=%fused_computation.51 | custom fusion | flops 131072 | bytes 66048 | tf_op jit(solution)/shard_map/scatter-add | solution.py:77
  94.1 0.2 copy.173
  94.3 0.2 fusion.65
  94.6 1.3 collective-permute-start.5
  95.9 7.3 %collective-permute-start.4 = (bf16[1,128,16]{1,2,0:T(8,128)(2,1)S(1)}, bf16[1,128,16]{1,2,0:T(8,128)(2,1)S(1)}, u32[]{:S(2)}, u32[]{:S(2)}) collective-permute-start(bf16[1,128,16]{1,2,0:T(8,128)(2,1)S(1)} %get-tuple-element.18), channel_id=1, source_target_pairs={{0,4},{4,8},{8,12},{12,16},{16,20},{20,24},{24,28},{28,32},{32,36}... | collective-permute-start | bytes 12296 | tf_op jit(solution)/shard_map/ppermute | solution.py:16
  103.2 0.2 fusion.15
  103.4 0.6 collective-permute-done.4
  104.0 0.2 fusion.1
  104.3 0.2 fusion.66
  104.5 1.3 collective-permute-start.7
  105.8 4.2 %collective-permute-start.6 = (bf16[1,128,16]{1,2,0:T(8,128)(2,1)S(1)}, bf16[1,128,16]{1,2,0:T(8,128)(2,1)S(1)}, u32[]{:S(2)}, u32[]{:S(2)}) collective-permute-start(bf16[1,128,16]{1,2,0:T(8,128)(2,1)S(1)} %get-tuple-element.16), channel_id=1, source_target_pairs={{0,4},{4,8},{8,12},{12,16},{16,20},{20,24},{24,28},{28,32},{32,36}... | collective-permute-start | bytes 12296 | tf_op jit(solution)/shard_map/ppermute | solution.py:16
  110.1 0.2 fusion.13
  110.3 0.6 collective-permute-done.6
  110.8 0.2 fusion.3
  111.1 0.2 copy.202
  111.3 0.9 bitcast_subtract_fusion.3
  112.2 6.4 %scatter_custom_fusion.1 = f32[256,16]{1,0:T(8,128)S(1)} fusion(s32[1024]{0:T(1024)S(1)} %get-tuple-element.13, f32[1024,16]{1,0:T(8,128)} %bitcast_subtract_fusion.3, f32[]{:T(128)} %constant.25.clone.1), kind=kCustom, calls=%fused_computation.70 | custom fusion | flops 16384 | bytes 16896 | tf_op jit(solution)/shard_map/scatter-add | solution.py:81
  118.6 2.5 collective-permute-start.8
  121.1 0.9 collective-permute-done.8
  122.0 65.2 %all_gather.6 = f32[8192,16]{1,0:T(8,128)S(1)} all-gather(f32[128,16]{1,0:T(8,128)S(1)} %select_add_fusion), channel_id=1, replica_groups=mesh['rows'=64,'cols'=4] {'rows'}, dimensions={0}, use_global_device_ids=true | all-gather | bytes 532480 | tf_op jit(solution)/shard_map/all_gather | solution.py:88
  187.2 6.6 %convolution_bitcast_fusion.4 = f32[128,16]{0,1:T(8,128)S(1)} fusion(f32[8192,16]{1,0:T(8,128)S(1)} %all_gather.6, f32[128,8192]{1,0:T(8,128)S(1)} %copy-done.2), kind=kOutput, calls=%fused_computation.22 | convolution fusion | flops 201326592 | bytes 4726784 | tf_op jit(solution)/shard_map/dot_general | solution.py:86
  193.8 0.4 collective-permute-start.9
  194.2 0.8 collective-permute-done.9
  195.0 0.1 copy.186
  195.1 2.8 gather_fusion.4
  197.9 0.2 copy.187
  198.2 0.2 fusion.67
  198.4 1.3 collective-permute-start.11
  199.7 3.0 collective-permute-start.10
  202.8 0.2 fusion.11
  203.0 0.6 collective-permute-done.10
  203.6 0.2 fusion.5
  203.8 0.2 copy.193
  204.0 27.9 %gather_fusion.5 = f32[8192,16]{1,0:T(8,128)} fusion(f32[1024,16]{1,0:T(8,128)S(1)} %copy.193, s32[8192]{0:T(1024)S(1)} %get-tuple-element.10), kind=kCustom, calls=%fused_computation.5 | custom fusion | bytes 1081344 | tf_op jit(solution)/shard_map/gather | solution.py:100
  231.9 2.8 copy.194
  234.7 0.1 copy_bitcast_fusion
  234.8 3.4 collective-permute-start.12
  238.3 1.3 collective-permute-start.13
  239.6 3.9 collective-permute-done.13
  243.6 0.8 gather_fusion.6
  244.4 5.7 %convolution_bitcast_fusion = f32[64,2,8,128]{3,2,1,0:T(8,128)S(1)} fusion(bf16[64,4,128,16]{2,3,1,0:T(8,128)(2,1)S(1)} %bitcast.176, bf16[64,4,128,128]{3,2,1,0:T(8,128)(2,1)} %param.10), kind=kOutput, calls=%fused_computation.9 | convolution fusion | flops 134217728 | bytes 9961472 | tf_op jit(solution)/shard_map/bkij,bkjc->bic/dot_general | solution.py:33
  250.1 0.2 fusion.7
  250.3 18.4 %all-gather.2.cloned.1.call-done = bf16[8192,64]{0,1:T(8,128)(2,1)} async-done(((bf16[8192,16]{0,1:T(8,128)(2,1)}), bf16[8192,64]{0,1:T(8,128)(2,1)}) %all-gather.2.cloned.1.call-update) | async-done | bytes 1048592 | tf_op jit(solution)/shard_map/all_gather | solution.py:106
  268.7 1.6 convolution_bitcast_fusion.3
  270.3 130.8 %psum.7 = f32[64,16]{0,1:T(8,128)} all-reduce(f32[64,16]{0,1:T(8,128)S(1)} %convolution_bitcast_fusion.3), channel_id=1, replica_groups=mesh['rows'=64,'cols'=4] {'rows'}, use_global_device_ids=true, to_apply=%region_2.3 | all-reduce | flops 1024 | bytes 8192 | tf_op jit(solution)/shard_map/psum | solution.py:111
  (51 shorter events, 0.9 us)
Async XLA Ops:
  7.2 1.6 slice-start
  7.2 261.5 %all-gather.2.cloned.1.call-start = ((), (), s32[]{:S(2)}) async-start(), calls=%async_computation | async-start | bytes 1310720 | tf_op jit(solution)/shard_map/all_gather | solution.py:106
  8.8 6.0 %copy-start = (f32[8192,16]{0,1:T(8,128)S(1)}, f32[8192,16]{0,1:T(8,128)}, u32[]{:S(2)}) copy-start(f32[8192,16]{0,1:T(8,128)} %param.8) | copy-start | bytes 1572868
  8.8 9.1 %copy-start.6 = (s32[64,4]{0,1:T(4,128)S(1)}, s32[64,4]{0,1:T(4,128)}, u32[]{:S(2)}) copy-start(s32[64,4]{0,1:T(4,128)} %param.11) | copy-start | bytes 3076
  12.7 11.5 %copy-start.5 = (s32[1024]{0:T(1024)S(1)}, s32[1024]{0:T(1024)}, u32[]{:S(2)}) copy-start(s32[1024]{0:T(1024)} %param.14) | copy-start | bytes 12292
  14.8 9.4 %collective-permute-start = (bf16[64,128,16]{1,2,0:T(8,128)(2,1)S(1)}, bf16[64,128,16]{1,2,0:T(8,128)(2,1)S(1)}, u32[]{:S(2)}, u32[]{:S(2)}) collective-permute-start(bf16[64,128,16]{1,2,0:T(8,128)(2,1)S(1)} %copy_bitcast_fusion.2), channel_id=1, source_target_pairs={{0,4},{4,8},{8,12},{12,16},{16,20},{20,24},{24,28},{28,32},{32,36}... | collective-permute-start | bytes 786440 | tf_op jit(solution)/shard_map/ppermute | solution.py:16
  16.5 7.7 %collective-permute-start.1 = (bf16[64,128,16]{1,2,0:T(8,128)(2,1)S(1)}, bf16[64,128,16]{1,2,0:T(8,128)(2,1)S(1)}, u32[]{:S(2)}, u32[]{:S(2)}) collective-permute-start(bf16[64,128,16]{1,2,0:T(8,128)(2,1)S(1)} %copy_bitcast_fusion.2), channel_id=1, source_target_pairs={{4,0},{8,4},{12,8},{16,12},{20,16},{24,20},{28,24},{32,28},{36,32}... | collective-permute-start | bytes 786440 | tf_op jit(solution)/shard_map/ppermute | solution.py:17
  25.2 11.9 %copy-start.4 = (s32[8192]{0:T(1024)S(1)}, s32[8192]{0:T(1024)}, u32[]{:S(2)}) copy-start(s32[8192]{0:T(1024)} %param.13) | copy-start | bytes 98308
  31.0 6.1 %collective-permute-start.2 = (bf16[64,128,16]{1,2,0:T(8,128)(2,1)S(1)}, bf16[64,128,16]{1,2,0:T(8,128)(2,1)S(1)}, u32[]{:S(2)}, u32[]{:S(2)}) collective-permute-start(bf16[64,128,16]{1,2,0:T(8,128)(2,1)S(1)} %copy_bitcast_fusion.1), channel_id=1, source_target_pairs={{0,4},{4,8},{8,12},{12,16},{16,20},{20,24},{24,28},{28,32},{32,36}... | collective-permute-start | bytes 786440 | tf_op jit(solution)/shard_map/ppermute | solution.py:16
  35.7 4.7 %collective-permute-start.3 = (bf16[64,128,16]{1,2,0:T(8,128)(2,1)S(1)}, bf16[64,128,16]{1,2,0:T(8,128)(2,1)S(1)}, u32[]{:S(2)}, u32[]{:S(2)}) collective-permute-start(bf16[64,128,16]{1,2,0:T(8,128)(2,1)S(1)} %copy_bitcast_fusion.1), channel_id=1, source_target_pairs={{4,0},{8,4},{12,8},{16,12},{20,16},{24,20},{28,24},{32,28},{36,32}... | collective-permute-start | bytes 786440 | tf_op jit(solution)/shard_map/ppermute | solution.py:17
  47.0 47.3 %copy-start.1 = (bf16[8,3,128,128]{3,2,1,0:T(8,128)(2,1)S(1)}, bf16[8,3,128,128]{3,2,1,0:T(8,128)(2,1)}, u32[]{:S(2)}) copy-start(bf16[8,3,128,128]{3,2,1,0:T(8,128)(2,1)} %param.12) | copy-start | bytes 2359300
  94.6 8.6 %collective-permute-start.5 = (bf16[1,128,16]{1,2,0:T(8,128)(2,1)S(1)}, bf16[1,128,16]{1,2,0:T(8,128)(2,1)S(1)}, u32[]{:S(2)}, u32[]{:S(2)}) collective-permute-start(bf16[1,128,16]{1,2,0:T(8,128)(2,1)S(1)} %get-tuple-element.19), channel_id=1, source_target_pairs={{4,0},{8,4},{12,8},{16,12},{20,16},{24,20},{28,24},{32,28},{36,32}... | collective-permute-start | bytes 12296 | tf_op jit(solution)/shard_map/ppermute | solution.py:17
  95.9 8.1 %collective-permute-start.4 = (bf16[1,128,16]{1,2,0:T(8,128)(2,1)S(1)}, bf16[1,128,16]{1,2,0:T(8,128)(2,1)S(1)}, u32[]{:S(2)}, u32[]{:S(2)}) collective-permute-start(bf16[1,128,16]{1,2,0:T(8,128)(2,1)S(1)} %get-tuple-element.18), channel_id=1, source_target_pairs={{0,4},{4,8},{8,12},{12,16},{16,20},{20,24},{24,28},{28,32},{32,36}... | collective-permute-start | bytes 12296 | tf_op jit(solution)/shard_map/ppermute | solution.py:16
  104.5 5.5 %collective-permute-start.7 = (bf16[1,128,16]{1,2,0:T(8,128)(2,1)S(1)}, bf16[1,128,16]{1,2,0:T(8,128)(2,1)S(1)}, u32[]{:S(2)}, u32[]{:S(2)}) collective-permute-start(bf16[1,128,16]{1,2,0:T(8,128)(2,1)S(1)} %get-tuple-element.17), channel_id=1, source_target_pairs={{4,0},{8,4},{12,8},{16,12},{20,16},{24,20},{28,24},{32,28},{36,32}... | collective-permute-start | bytes 12296 | tf_op jit(solution)/shard_map/ppermute | solution.py:17
  105.8 5.0 %collective-permute-start.6 = (bf16[1,128,16]{1,2,0:T(8,128)(2,1)S(1)}, bf16[1,128,16]{1,2,0:T(8,128)(2,1)S(1)}, u32[]{:S(2)}, u32[]{:S(2)}) collective-permute-start(bf16[1,128,16]{1,2,0:T(8,128)(2,1)S(1)} %get-tuple-element.16), channel_id=1, source_target_pairs={{0,4},{4,8},{8,12},{12,16},{16,20},{20,24},{24,28},{28,32},{32,36}... | collective-permute-start | bytes 12296 | tf_op jit(solution)/shard_map/ppermute | solution.py:16
  118.6 68.6 %copy-start.2 = (f32[128,8192]{1,0:T(8,128)S(1)}, f32[128,8192]{1,0:T(8,128)}, u32[]{:S(2)}) copy-start(f32[128,8192]{1,0:T(8,128)} %param.15) | copy-start | bytes 12582916
  118.6 3.4 collective-permute-start.8
  193.8 1.2 collective-permute-start.9
  198.4 4.4 %collective-permute-start.11 = (bf16[1,128,16]{1,2,0:T(8,128)(2,1)S(1)}, bf16[1,128,16]{1,2,0:T(8,128)(2,1)S(1)}, u32[]{:S(2)}, u32[]{:S(2)}) collective-permute-start(bf16[1,128,16]{1,2,0:T(8,128)(2,1)S(1)} %get-tuple-element.15), channel_id=1, source_target_pairs={{4,0},{8,4},{12,8},{16,12},{20,16},{24,20},{28,24},{32,28},{36,32}... | collective-permute-start | bytes 12296 | tf_op jit(solution)/shard_map/ppermute | solution.py:17
  199.7 3.8 collective-permute-start.10
  234.8 4.8 %collective-permute-start.12 = (bf16[64,128,16]{1,2,0:T(8,128)(2,1)S(1)}, bf16[64,128,16]{1,2,0:T(8,128)(2,1)S(1)}, u32[]{:S(2)}, u32[]{:S(2)}) collective-permute-start(bf16[64,128,16]{1,2,0:T(8,128)(2,1)S(1)} %copy_bitcast_fusion), channel_id=1, source_target_pairs={{0,4},{4,8},{8,12},{12,16},{16,20},{20,24},{24,28},{28,32},{32,36}... | collective-permute-start | bytes 786440 | tf_op jit(solution)/shard_map/ppermute | solution.py:16
  238.3 5.2 %collective-permute-start.13 = (bf16[64,128,16]{1,2,0:T(8,128)(2,1)S(1)}, bf16[64,128,16]{1,2,0:T(8,128)(2,1)S(1)}, u32[]{:S(2)}, u32[]{:S(2)}) collective-permute-start(bf16[64,128,16]{1,2,0:T(8,128)(2,1)S(1)} %copy_bitcast_fusion), channel_id=1, source_target_pairs={{4,0},{8,4},{12,8},{16,12},{20,16},{24,20},{28,24},{32,28},{36,32}... | collective-permute-start | bytes 786440 | tf_op jit(solution)/shard_map/ppermute | solution.py:17
  250.3 150.8 %copy-start.3 = (f32[8192,16]{0,1:T(8,128)}, f32[8192,16]{0,1:T(8,128)S(1)}, u32[]{:S(2)}) copy-start(f32[8192,16]{0,1:T(8,128)S(1)} %fusion.7) | copy-start | bytes 1572868
Sparse Core Ops, SparseCore 0:
  239.7 28.9 all-gather.1
where the time goes:
time: 409 us; the launch traced here: 408 us
  blocking collectives  196 us (48%)
  local copies, waits for them, and re-layouts  53.3 us (13%)
  other arithmetic  52.8 us (13%)
  starting transfers between devices  35.1 us (9%)
  waiting for transfers between devices  29 us (7%)
  matrix products  27.3 us (7%)
  between operations  14.5 us (4%)
    psum x1, blocking collectives, on_device(): gram = lax.psum(partial_gram, 'rows')  131 us
    all_gather x1, blocking collectives, on_device(): lax.all_gather(coarse_rhs, 'rows', axis=0, tiled=True)  65.2 us
    scatter-add x1, other arithmetic, on_device(): jax.ops.segment_sum(fine_res, fine_local, num_segments=mid_count)  44.4 us
    gather x2, local copies, waits for them, and re-layouts, on_device(): fine_x = fine_x + mid_x[fine_local]  30.7 us
    ppermute x6, starting transfers between devices, with_halo(): before = lax.ppermute(last, axis, up)  24.4 us
    all_gather x1, waiting for transfers between devices, on_device(): lax.all_gather(basis, 'cols', axis=1, tiled=True)  18.4 us
    dot_general x3, matrix products, fine_apply(): jnp.einsum('bkij,bkjc->bic', matrix, picked, preferred_element_type=jnp.f...  17 us
  transfers between devices with their start and end apart: 15, of which 8 were waited for; matrix products, arithmetic and copies ran while one was open for 3% of the time, Pallas kernels for 0%

commit v1 on v0

--- a/solution.py
+++ b/solution.py
@@ -4,6 +4,25 @@
 from jax.sharding import PartitionSpec as P
 
 DAMPING = 0.6666666666666666
+
+
+def ring_gather(value, axis, dim):
+    size, place, span = (lax.axis_size(axis), lax.axis_index(axis), value.shape[dim])
+    right = [(i, (i + 1) % size) for i in range(size)]
+    left = [(i, (i - 1) % size) for i in range(size)]
+    out = jnp.zeros((*value.shape[:dim], size * span, *value.shape[dim + 1 :]), value.dtype)
+    out = lax.dynamic_update_slice_in_dim(out, value, place * span, axis=dim)
+    from_left = from_right = value
+    half = size // 2
+    for hop in range(1, half + 1):
+        from_left = lax.ppermute(from_left, axis, right)
+        out = lax.dynamic_update_slice_in_dim(out, from_left, (place - hop) % size * span, axis=dim)
+        if hop < size - half:
+            from_right = lax.ppermute(from_right, axis, left)
+            out = lax.dynamic_update_slice_in_dim(
+                out, from_right, (place + hop) % size * span, axis=dim
+            )
+    return out
 
 
 def with_halo(array, sides, width):
@@ -103,7 +122,7 @@
     )
     rounded = finished.astype(jnp.bfloat16)
     partial_gram = lax.dot_general(
-        lax.all_gather(basis, "cols", axis=1, tiled=True),
+        ring_gather(basis, "cols", 1),
         rounded,
         (((0,), (0,)), ((), ())),
         preferred_element_type=jnp.float32,

time: 409 us -> 381 us (0.932)
  waiting for transfers between devices: 29 us -> 6.02 us
  between operations: 14.5 us -> 1.22 us
  local copies, waits for them, and re-layouts: 53.3 us -> 59.4 us
    all_gather x1 -> x0, waiting for transfers between devices: 18.4 us -> none  [on_device(): lax.all_gather(basis, 'cols', axis=1, tiled=True)]
    dynamic_update_slice x0 -> x4, local copies, waits for them, and re-layouts: none -> 6.05 us  [the longest x2 3.38 us: ring_gather(): lax.dynamic_update_slice_in_dim(out, from_left, (place - hop) % size * sp...]
  transfers between devices with their start and end apart: 15 -> 17, of which waited for: 8 -> 5; matrix products, arithmetic and copies ran while one was open for 3% -> 32% of each run, Pallas kernels for 0% -> 0%
where the time goes in v1:
time: 381 us; the launch traced here: 380 us
  blocking collectives  196 us (51%)
  local copies, waits for them, and re-layouts  59.4 us (16%)
  other arithmetic  52.8 us (14%)
  starting transfers between devices  37.9 us (10%)
  matrix products  26.2 us (7%)
  waiting for transfers between devices  6.02 us (2%)
    psum x1, blocking collectives, on_device(): gram = lax.psum(partial_gram, 'rows')  131 us
    all_gather x1, blocking collectives, on_device(): lax.all_gather(coarse_rhs, 'rows', axis=0, tiled=True)  65.1 us
    scatter-add x1, other arithmetic, on_device(): jax.ops.segment_sum(fine_res, fine_local, num_segments=mid_count)  44.4 us
    gather x2, local copies, waits for them, and re-layouts, on_device(): fine_x = fine_x + mid_x[fine_local]  30.6 us
    ppermute x6, starting transfers between devices, with_halo(): before = lax.ppermute(last, axis, up)  24.1 us
    dot_general x3, matrix products, fine_apply(): jnp.einsum('bkij,bkjc->bic', matrix, picked, preferred_element_type=jnp.f...  17.1 us
    ppermute x6, starting transfers between devices, with_halo(): after = lax.ppermute(leading, axis, down)  7.78 us
  transfers between devices with their start and end apart: 17, of which 5 were waited for; matrix products, arithmetic and copies ran while one was open for 32% of the time, Pallas kernels for 0%

profile of v1, /device:TPU:4, one launch (start us, length us, event | category | flops | bytes accessed | tf_op | source)
XLA Modules:
  0.0 380.0 jit_solution(5236980980485462611)
XLA Ops:
  0.7 1.6 slice-done
  2.2 3.9 %copy.204 = bf16[64,1,128,128]{0,3,2,1:T(8,128)(2,1)} copy(bf16[64,1,128,128]{3,2,1,0:T(8,128)(2,1)S(1)} %slice-done) | data formatting | bytes 4194304
  6.1 2.0 gather_fusion
  8.3 1.8 collective-permute-start
  10.0 1.3 collective-permute-start.1
  11.3 1.3 collective-permute-start.14
  12.6 0.8 collective-permute-start.15
  13.6 1.0 slice_bitcast_fusion
  14.7 1.0 constant_dynamic-update-slice_fusion.3
  15.7 3.1 copy.166
  18.8 2.0 gather_fusion.2
  21.0 0.8 gather_fusion.1
  21.8 5.7 %convolution_bitcast_fusion.2 = f32[64,2,8,128]{3,2,1,0:T(8,128)S(1)} fusion(bf16[64,4,128,16]{2,3,1,0:T(8,128)(2,1)S(1)} %bitcast.175, bf16[64,4,128,128]{3,2,1,0:T(8,128)(2,1)} %param.10), kind=kOutput, calls=%fused_computation.11 | convolution fusion | flops 134217728 | bytes 9961472 | tf_op jit(solution)/shard_map/bkij,bkjc->bic/dot_general | solution.py:52
  27.6 4.2 %collective-permute-start.2 = (bf16[64,128,16]{1,2,0:T(8,128)(2,1)S(1)}, bf16[64,128,16]{1,2,0:T(8,128)(2,1)S(1)}, u32[]{:S(2)}, u32[]{:S(2)}) collective-permute-start(bf16[64,128,16]{1,2,0:T(8,128)(2,1)S(1)} %copy_bitcast_fusion.1), channel_id=1, source_target_pairs={{0,4},{4,8},{8,12},{12,16},{16,20},{20,24},{24,28},{28,32},{32,36}... | collective-permute-start | bytes 786440 | tf_op jit(solution)/shard_map/ppermute | solution.py:35
  31.8 1.3 collective-permute-start.3
  33.2 1.3 collective-permute-start.16
  34.5 2.5 collective-permute-done.3
  37.1 0.8 gather_fusion.3
  38.0 5.7 %convolution_bitcast_fusion.1 = f32[64,2,8,128]{3,2,1,0:T(8,128)S(1)} fusion(bf16[64,4,128,16]{2,3,1,0:T(8,128)(2,1)S(1)} %bitcast.176, bf16[64,4,128,128]{3,2,1,0:T(8,128)(2,1)} %param.10), kind=kOutput, calls=%fused_computation.10 | convolution fusion | flops 134217728 | bytes 9961472 | tf_op jit(solution)/shard_map/bkij,bkjc->bic/dot_general | solution.py:52
  43.7 2.6 copy.172
  46.3 44.4 %scatter_custom_fusion = f32[1024,16]{1,0:T(8,128)S(1)} fusion(s32[8192]{0:T(1024)S(1)} %get-tuple-element.11, f32[8192,16]{1,0:T(8,128)} %copy.172, f32[]{:T(128)} %constant.71.clone.1), kind=kCustom, calls=%fused_computation.51 | custom fusion | flops 131072 | bytes 66048 | tf_op jit(solution)/shard_map/scatter-add | solution.py:96
  90.8 0.2 copy.173
  91.0 0.2 fusion.66
  91.2 1.3 collective-permute-start.5
  92.5 7.3 %collective-permute-start.4 = (bf16[1,128,16]{1,2,0:T(8,128)(2,1)S(1)}, bf16[1,128,16]{1,2,0:T(8,128)(2,1)S(1)}, u32[]{:S(2)}, u32[]{:S(2)}) collective-permute-start(bf16[1,128,16]{1,2,0:T(8,128)(2,1)S(1)} %get-tuple-element.18), channel_id=1, source_target_pairs={{0,4},{4,8},{8,12},{12,16},{16,20},{20,24},{24,28},{28,32},{32,36}... | collective-permute-start | bytes 12296 | tf_op jit(solution)/shard_map/ppermute | solution.py:35
  99.8 0.2 fusion.15
  100.1 0.6 collective-permute-done.4
  100.6 0.2 fusion.1
  100.9 0.2 fusion.67
  101.2 1.3 collective-permute-start.7
  102.5 4.4 %collective-permute-start.6 = (bf16[1,128,16]{1,2,0:T(8,128)(2,1)S(1)}, bf16[1,128,16]{1,2,0:T(8,128)(2,1)S(1)}, u32[]{:S(2)}, u32[]{:S(2)}) collective-permute-start(bf16[1,128,16]{1,2,0:T(8,128)(2,1)S(1)} %get-tuple-element.16), channel_id=1, source_target_pairs={{0,4},{4,8},{8,12},{12,16},{16,20},{20,24},{24,28},{28,32},{32,36}... | collective-permute-start | bytes 12296 | tf_op jit(solution)/shard_map/ppermute | solution.py:35
  106.9 0.2 fusion.13
  107.1 0.4 collective-permute-done.6
  107.5 0.2 fusion.3
  107.7 0.2 copy.202
  107.9 0.9 bitcast_subtract_fusion.3
  108.8 6.4 %scatter_custom_fusion.1 = f32[256,16]{1,0:T(8,128)S(1)} fusion(s32[1024]{0:T(1024)S(1)} %get-tuple-element.13, f32[1024,16]{1,0:T(8,128)} %bitcast_subtract_fusion.3, f32[]{:T(128)} %constant.71.clone.1), kind=kCustom, calls=%fused_computation.70 | custom fusion | flops 16384 | bytes 16896 | tf_op jit(solution)/shard_map/scatter-add | solution.py:100
  115.3 2.3 collective-permute-start.8
  117.6 1.7 constant_dynamic-update-slice_fusion.2
  119.3 65.1 %all_gather.3 = f32[8192,16]{1,0:T(8,128)S(1)} all-gather(f32[128,16]{1,0:T(8,128)S(1)} %select_add_fusion), channel_id=1, replica_groups=mesh['rows'=64,'cols'=4] {'rows'}, dimensions={0}, use_global_device_ids=true | all-gather | bytes 532480 | tf_op jit(solution)/shard_map/all_gather | solution.py:107
  184.4 6.6 %convolution_bitcast_fusion.3 = f32[128,16]{0,1:T(8,128)S(1)} fusion(f32[8192,16]{1,0:T(8,128)S(1)} %all_gather.3, f32[128,8192]{1,0:T(8,128)S(1)} %copy-done.2), kind=kOutput, calls=%fused_computation.21 | convolution fusion | flops 201326592 | bytes 4726784 | tf_op jit(solution)/shard_map/dot_general | solution.py:105
  191.0 0.4 collective-permute-start.9
  191.3 1.7 constant_dynamic-update-slice_fusion.1
  193.1 2.8 gather_fusion.4
  196.0 0.2 copy.187
  196.2 0.2 fusion.68
  196.4 1.3 collective-permute-start.11
  197.7 3.3 collective-permute-start.10
  201.0 0.2 fusion.11
  201.2 0.3 collective-permute-done.10
  201.6 0.2 fusion.5
  201.8 0.2 copy.193
  202.0 27.8 %gather_fusion.5 = f32[8192,16]{1,0:T(8,128)} fusion(f32[1024,16]{1,0:T(8,128)S(1)} %copy.193, s32[8192]{0:T(1024)S(1)} %get-tuple-element.10), kind=kCustom, calls=%fused_computation.5 | custom fusion | bytes 1081344 | tf_op jit(solution)/shard_map/gather | solution.py:119
  229.9 2.8 copy.194
  232.7 0.1 copy_bitcast_fusion
  232.8 3.2 collective-permute-start.12
  236.1 1.3 collective-permute-start.13
  237.4 1.7 constant_dynamic-update-slice_fusion
  239.1 2.2 collective-permute-done.13
  241.4 0.8 gather_fusion.6
  242.2 5.7 %convolution_bitcast_fusion = f32[64,2,8,128]{3,2,1,0:T(8,128)S(1)} fusion(bf16[64,4,128,16]{2,3,1,0:T(8,128)(2,1)S(1)} %bitcast.174, bf16[64,4,128,128]{3,2,1,0:T(8,128)(2,1)} %param.10), kind=kOutput, calls=%fused_computation.9 | convolution fusion | flops 134217728 | bytes 9961472 | tf_op jit(solution)/shard_map/bkij,bkjc->bic/dot_general | solution.py:52
  248.0 0.2 fusion.7
  248.2 0.4 fusion.20
  248.6 131.4 %psum.7 = f32[64,16]{0,1:T(8,128)} all-reduce(f32[64,16]{0,1:T(8,128)S(1)} %fusion.20), channel_id=1, replica_groups=mesh['rows'=64,'cols'=4] {'rows'}, use_global_device_ids=true, to_apply=%region_2.3 | all-reduce | flops 1024 | bytes 8192 | tf_op jit(solution)/shard_map/psum | solution.py:130
  (63 shorter events, 1.4 us)
Async XLA Ops:
  0.6 1.6 slice-start
  2.2 6.0 %copy-start = (f32[8192,16]{0,1:T(8,128)S(1)}, f32[8192,16]{0,1:T(8,128)}, u32[]{:S(2)}) copy-start(f32[8192,16]{0,1:T(8,128)} %param.8) | copy-start | bytes 1572868
  2.2 11.2 %copy-start.8 = (s32[64,4]{0,1:T(4,128)S(1)}, s32[64,4]{0,1:T(4,128)}, u32[]{:S(2)}) copy-start(s32[64,4]{0,1:T(4,128)} %param.11) | copy-start | bytes 3076
  6.1 14.7 %copy-start.7 = (s32[1024]{0:T(1024)S(1)}, s32[1024]{0:T(1024)}, u32[]{:S(2)}) copy-start(s32[1024]{0:T(1024)} %param.14) | copy-start | bytes 12292
  8.3 12.6 %collective-permute-start = (bf16[64,128,16]{1,2,0:T(8,128)(2,1)S(1)}, bf16[64,128,16]{1,2,0:T(8,128)(2,1)S(1)}, u32[]{:S(2)}, u32[]{:S(2)}) collective-permute-start(bf16[64,128,16]{1,2,0:T(8,128)(2,1)S(1)} %copy_bitcast_fusion.2), channel_id=1, source_target_pairs={{0,4},{4,8},{8,12},{12,16},{16,20},{20,24},{24,28},{28,32},{32,36}... | collective-permute-start | bytes 786440 | tf_op jit(solution)/shard_map/ppermute | solution.py:35
  10.0 10.9 %collective-permute-start.1 = (bf16[64,128,16]{1,2,0:T(8,128)(2,1)S(1)}, bf16[64,128,16]{1,2,0:T(8,128)(2,1)S(1)}, u32[]{:S(2)}, u32[]{:S(2)}) collective-permute-start(bf16[64,128,16]{1,2,0:T(8,128)(2,1)S(1)} %copy_bitcast_fusion.2), channel_id=1, source_target_pairs={{4,0},{8,4},{12,8},{16,12},{20,16},{24,20},{28,24},{32,28},{36,32}... | collective-permute-start | bytes 786440 | tf_op jit(solution)/shard_map/ppermute | solution.py:36
  11.3 21.9 %collective-permute-start.14 = (bf16[8192,16]{0,1:T(8,128)(2,1)}, bf16[8192,16]{0,1:T(8,128)(2,1)}, u32[]{:S(2)}, u32[]{:S(2)}) collective-permute-start(bf16[8192,16]{0,1:T(8,128)(2,1)} %param.9), channel_id=1, source_target_pairs={{0,1},{1,2},{2,3},{3,0},{4,5},{5,6},{6,7},{7,4},{8,9},{9,10},{10,1... | collective-permute-start | bytes 786440 | tf_op jit(solution)/shard_map/ppermute | solution.py:18
  12.6 178.7 %collective-permute-start.15 = (bf16[8192,16]{0,1:T(8,128)(2,1)}, bf16[8192,16]{0,1:T(8,128)(2,1)}, u32[]{:S(2)}, u32[]{:S(2)}) collective-permute-start(bf16[8192,16]{0,1:T(8,128)(2,1)} %param.9), channel_id=1, source_target_pairs={{0,3},{1,0},{2,1},{3,2},{4,7},{5,4},{6,5},{7,6},{8,11},{9,8},{10,9... | collective-permute-start | bytes 786440 | tf_op jit(solution)/shard_map/ppermute | solution.py:21
  15.7 5.2 %copy-start.3 = (bf16[8192,64]{0,1:T(8,128)(2,1)}, bf16[8192,64]{0,1:T(8,128)(2,1)S(1)}, u32[]{:S(2)}) copy-start(bf16[8192,64]{0,1:T(8,128)(2,1)S(1)} %constant_dynamic-update-slice_fusion.3) | copy-start | bytes 3145732
  21.8 11.4 %copy-start.6 = (s32[8192]{0:T(1024)S(1)}, s32[8192]{0:T(1024)}, u32[]{:S(2)}) copy-start(s32[8192]{0:T(1024)} %param.13) | copy-start | bytes 98308
  27.6 6.9 %collective-permute-start.2 = (bf16[64,128,16]{1,2,0:T(8,128)(2,1)S(1)}, bf16[64,128,16]{1,2,0:T(8,128)(2,1)S(1)}, u32[]{:S(2)}, u32[]{:S(2)}) collective-permute-start(bf16[64,128,16]{1,2,0:T(8,128)(2,1)S(1)} %copy_bitcast_fusion.1), channel_id=1, source_target_pairs={{0,4},{4,8},{8,12},{12,16},{16,20},{20,24},{24,28},{28,32},{32,36}... | collective-permute-start | bytes 786440 | tf_op jit(solution)/shard_map/ppermute | solution.py:35
  31.8 5.2 %collective-permute-start.3 = (bf16[64,128,16]{1,2,0:T(8,128)(2,1)S(1)}, bf16[64,128,16]{1,2,0:T(8,128)(2,1)S(1)}, u32[]{:S(2)}, u32[]{:S(2)}) collective-permute-start(bf16[64,128,16]{1,2,0:T(8,128)(2,1)S(1)} %copy_bitcast_fusion.1), channel_id=1, source_target_pairs={{4,0},{8,4},{12,8},{16,12},{20,16},{24,20},{28,24},{32,28},{36,32}... | collective-permute-start | bytes 786440 | tf_op jit(solution)/shard_map/ppermute | solution.py:36
  33.2 204.1 %collective-permute-start.16 = (bf16[8192,16]{0,1:T(8,128)(2,1)}, bf16[8192,16]{0,1:T(8,128)(2,1)}, u32[]{:S(2)}, u32[]{:S(2)}) collective-permute-start(bf16[8192,16]{0,1:T(8,128)(2,1)} %collective-permute-done.14), channel_id=1, source_target_pairs={{0,1},{1,2},{2,3},{3,0},{4,5},{5,6},{6,7},{7,4},{8,9},{9,10},{10,1... | collective-permute-start | bytes 786440 | tf_op jit(solution)/shard_map/ppermute | solution.py:18
  43.6 47.3 %copy-start.1 = (bf16[8,3,128,128]{3,2,1,0:T(8,128)(2,1)S(1)}, bf16[8,3,128,128]{3,2,1,0:T(8,128)(2,1)}, u32[]{:S(2)}) copy-start(bf16[8,3,128,128]{3,2,1,0:T(8,128)(2,1)} %param.12) | copy-start | bytes 2359300
  91.2 8.6 %collective-permute-start.5 = (bf16[1,128,16]{1,2,0:T(8,128)(2,1)S(1)}, bf16[1,128,16]{1,2,0:T(8,128)(2,1)S(1)}, u32[]{:S(2)}, u32[]{:S(2)}) collective-permute-start(bf16[1,128,16]{1,2,0:T(8,128)(2,1)S(1)} %get-tuple-element.19), channel_id=1, source_target_pairs={{4,0},{8,4},{12,8},{16,12},{20,16},{24,20},{28,24},{32,28},{36,32}... | collective-permute-start | bytes 12296 | tf_op jit(solution)/shard_map/ppermute | solution.py:36
  92.5 8.1 %collective-permute-start.4 = (bf16[1,128,16]{1,2,0:T(8,128)(2,1)S(1)}, bf16[1,128,16]{1,2,0:T(8,128)(2,1)S(1)}, u32[]{:S(2)}, u32[]{:S(2)}) collective-permute-start(bf16[1,128,16]{1,2,0:T(8,128)(2,1)S(1)} %get-tuple-element.18), channel_id=1, source_target_pairs={{0,4},{4,8},{8,12},{12,16},{16,20},{20,24},{24,28},{28,32},{32,36}... | collective-permute-start | bytes 12296 | tf_op jit(solution)/shard_map/ppermute | solution.py:35
  101.2 5.7 %collective-permute-start.7 = (bf16[1,128,16]{1,2,0:T(8,128)(2,1)S(1)}, bf16[1,128,16]{1,2,0:T(8,128)(2,1)S(1)}, u32[]{:S(2)}, u32[]{:S(2)}) collective-permute-start(bf16[1,128,16]{1,2,0:T(8,128)(2,1)S(1)} %get-tuple-element.17), channel_id=1, source_target_pairs={{4,0},{8,4},{12,8},{16,12},{20,16},{24,20},{28,24},{32,28},{36,32}... | collective-permute-start | bytes 12296 | tf_op jit(solution)/shard_map/ppermute | solution.py:36
  102.5 5.0 %collective-permute-start.6 = (bf16[1,128,16]{1,2,0:T(8,128)(2,1)S(1)}, bf16[1,128,16]{1,2,0:T(8,128)(2,1)S(1)}, u32[]{:S(2)}, u32[]{:S(2)}) collective-permute-start(bf16[1,128,16]{1,2,0:T(8,128)(2,1)S(1)} %get-tuple-element.16), channel_id=1, source_target_pairs={{0,4},{4,8},{8,12},{12,16},{16,20},{20,24},{24,28},{28,32},{32,36}... | collective-permute-start | bytes 12296 | tf_op jit(solution)/shard_map/ppermute | solution.py:35
  115.3 69.1 %copy-start.2 = (f32[128,8192]{1,0:T(8,128)S(1)}, f32[128,8192]{1,0:T(8,128)}, u32[]{:S(2)}) copy-start(f32[128,8192]{1,0:T(8,128)} %param.15) | copy-start | bytes 12582916
  115.3 4.0 %collective-permute-start.8 = (f32[128,16]{1,0:T(8,128)S(1)}, f32[128,16]{1,0:T(8,128)S(1)}, u32[]{:S(2)}, u32[]{:S(2)}) collective-permute-start(f32[128,16]{1,0:T(8,128)S(1)} %slice_select_fusion), channel_id=1, source_target_pairs={{0,4},{4,0},{8,12},{12,8},{16,20},{20,16},{24,28},{28,24},{32,36},... | collective-permute-start | bytes 24584 | tf_op jit(solution)/shard_map/ppermute | solution.py:44
  191.0 2.1 collective-permute-start.9
  196.4 4.6 %collective-permute-start.11 = (bf16[1,128,16]{1,2,0:T(8,128)(2,1)S(1)}, bf16[1,128,16]{1,2,0:T(8,128)(2,1)S(1)}, u32[]{:S(2)}, u32[]{:S(2)}) collective-permute-start(bf16[1,128,16]{1,2,0:T(8,128)(2,1)S(1)} %get-tuple-element.15), channel_id=1, source_target_pairs={{4,0},{8,4},{12,8},{16,12},{20,16},{24,20},{28,24},{32,28},{36,32}... | collective-permute-start | bytes 12296 | tf_op jit(solution)/shard_map/ppermute | solution.py:36
  197.7 3.8 %collective-permute-start.10 = (bf16[1,128,16]{1,2,0:T(8,128)(2,1)S(1)}, bf16[1,128,16]{1,2,0:T(8,128)(2,1)S(1)}, u32[]{:S(2)}, u32[]{:S(2)}) collective-permute-start(bf16[1,128,16]{1,2,0:T(8,128)(2,1)S(1)} %get-tuple-element.14), channel_id=1, source_target_pairs={{0,4},{4,8},{8,12},{12,16},{16,20},{20,24},{24,28},{28,32},{32,36}... | collective-permute-start | bytes 12296 | tf_op jit(solution)/shard_map/ppermute | solution.py:35
  232.8 6.3 %collective-permute-start.12 = (bf16[64,128,16]{1,2,0:T(8,128)(2,1)S(1)}, bf16[64,128,16]{1,2,0:T(8,128)(2,1)S(1)}, u32[]{:S(2)}, u32[]{:S(2)}) collective-permute-start(bf16[64,128,16]{1,2,0:T(8,128)(2,1)S(1)} %copy_bitcast_fusion), channel_id=1, source_target_pairs={{0,4},{4,8},{8,12},{12,16},{16,20},{20,24},{24,28},{28,32},{32,36}... | collective-permute-start | bytes 786440 | tf_op jit(solution)/shard_map/ppermute | solution.py:35
  236.1 5.2 %collective-permute-start.13 = (bf16[64,128,16]{1,2,0:T(8,128)(2,1)S(1)}, bf16[64,128,16]{1,2,0:T(8,128)(2,1)S(1)}, u32[]{:S(2)}, u32[]{:S(2)}) collective-permute-start(bf16[64,128,16]{1,2,0:T(8,128)(2,1)S(1)} %copy_bitcast_fusion), channel_id=1, source_target_pairs={{4,0},{8,4},{12,8},{16,12},{20,16},{24,20},{28,24},{32,28},{36,32}... | collective-permute-start | bytes 786440 | tf_op jit(solution)/shard_map/ppermute | solution.py:36
  242.2 6.0 %copy-start.4 = (bf16[8192,64]{0,1:T(8,128)(2,1)S(1)}, bf16[8192,64]{0,1:T(8,128)(2,1)}, u32[]{:S(2)}) copy-start(bf16[8192,64]{0,1:T(8,128)(2,1)} %constant_dynamic-update-slice_fusion) | copy-start | bytes 3145732
  248.2 131.8 %copy-start.5 = (f32[8192,16]{0,1:T(8,128)}, f32[8192,16]{0,1:T(8,128)S(1)}, u32[]{:S(2)}) copy-start(f32[8192,16]{0,1:T(8,128)S(1)} %fusion.7) | copy-start | bytes 1572868
